TPU v7x, 256 devices: a whole 4x4x8 slice. The times are simulated.
256 devices in a mesh: grp: 8 (over x, y_hi), band: 32 (over z, y_lo, core).
Axes of the slice: x: 4, y: 4 (y_hi: 2, y_lo: 2; y = y_hi * 2 + y_lo), z: 8, core: 2. Of those that a mesh axis runs over, the one named last changes fastest.
Arguments:
- orbitals: bfloat16 [128, 64, 4096], P('band'), may hold values from -6 to 6
Outputs:
- exchange: float32 [128, 64, 4096], P('band', 'grp')
All inputs are finite; a program needn't handle non-finite values.
Results may differ from a plain program's by a relative error of at most 0.0003.
Values may be sent and summed in bfloat16 or wider, within the bound.
No kernel may reach another device: no remote copies, remote signals or barrier semaphores. Data moves between devices by JAX's collectives and lax.ppermute only.
A program may use at most 128 MiB of HBM per device.

v0:
```python
import functools
import math

import jax
import jax.numpy as jnp
import ml_dtypes
import numpy as np
from jax import lax
from jax.experimental import pallas as pl
from jax.experimental.pallas import tpu as pltpu
from jax.sharding import PartitionSpec as P

CELL_LENGTH = 41.05
SCREENING = 0.106
G = 64
H = 128
T = 256


def split_table(m):
    hi = m.astype(ml_dtypes.bfloat16)
    lo = (m - hi.astype(np.float64)).astype(ml_dtypes.bfloat16)
    return np.block([[hi, hi], [lo, lo]])


def row_of(kind, r):
    s, kz, y = r % 8 // 4, r // 2 % 2, r % 2
    return 4 * (r // 8) + 2 * (s ^ kind) + y, 2 * kind + kz


def tables():
    i = np.arange(G)
    ang = 2 * np.pi * ((i[:, None] * i[None, :]) % G) / G
    h = (np.cos(ang) + np.sin(ang)) / 8.0
    r = np.arange(H)
    out = []
    for kind in range(2):
        kz = 4 * (r // 8) + 2 * ((r // 4 % 2) ^ kind) + r // 2 % 2
        m = (r[:, None] % 2 == r[None, :] // G) * h[kz[:, None], r[None, :] % G]
        out += [split_table(m), split_table(m.T)]
    for kind in range(2):
        y, kz = row_of(kind, r)
        out.append(split_table((kz[:, None] == kz[None, :]) * h[y[:, None], y[None, :]]))
    out.append(split_table(np.kron(np.eye(2), h)).T)
    return jnp.asarray(np.stack(out))


def kernel_table():
    s = (T // 8, H, H)
    j = lax.broadcasted_iota(jnp.int32, s, 0)
    r = lax.broadcasted_iota(jnp.int32, s, 1)
    l = lax.broadcasted_iota(jnp.int32, s, 2)

    def wave(k):
        return jnp.where(k < G // 2, k, k - G)

    y, kz = row_of(j % 2, r)
    a, b, c = wave(l % G), wave(y), wave(4 * (j // 2) + kz)
    q = (a * a + b * b + c * c).astype(jnp.float32)
    squared = q * (2.0 * math.pi / CELL_LENGTH) ** 2
    safe = jnp.where(squared > 0, squared, 1.0)
    screened = 4.0 * math.pi * (1.0 - jnp.exp(-safe / (4.0 * SCREENING * SCREENING))) / safe
    return -0.25 * jnp.where(squared > 0, screened, math.pi / (SCREENING * SCREENING))


NN = (((1,), (0,)), ((), ()))
NT = (((1,), (1,)), ((), ()))


def dot(a, b, dims):
    return lax.dot_general(a, b, dims, preferred_element_type=jnp.float32)


def split(v, axis):
    hi = v.astype(jnp.bfloat16)
    lo = (v - hi.astype(jnp.float32)).astype(jnp.bfloat16)
    return jnp.concatenate([hi, lo], axis=axis)


def pair_kernel(steps, first, *refs):
    ui, um, uo = steps
    own, pa, pb, pc, tabs, kt = refs[:6]
    acc = None if first else refs[6]
    out, buf = refs[-2:]
    zia, zoa, zib, zob, y0, y1, xw = (tabs.at[k] for k in range(7))
    n = T // 16
    low = lax.broadcasted_iota(jnp.int32, (n, 8, T), 1) < 4

    def lanes(t, size=T):
        return pl.ds(pl.multiple_of(t * size, size), size)

    def partners(t, size=T):
        return jnp.concatenate([p[:, :, lanes(t, size)] for p in (pa, pb, pc)], axis=0)

    def step_in(i, c):
        ts = [i * ui + k for k in range(ui)]

        def product(u):
            phi = own[:, :, lanes(u, H)].astype(jnp.float32)
            return split((partners(u, H).astype(jnp.float32) * phi).reshape(T, H), 1)

        ds = [(product(2 * t + s), (zia, zib)[s]) for t in ts for s in range(2)]
        vs = [dot(w[...], d, NT) for d, w in ds]
        vs = [(v[:H] + v[H:]).reshape(n, 8, T) for v in vs]
        for k, t in enumerate(ts):
            a, b = vs[2 * k], vs[2 * k + 1]
            buf[t] = jnp.stack([jnp.where(low, a, b), jnp.where(low, b, a)], axis=1).reshape(T, T)
        return c

    def along_x(vs):
        vs = [jnp.concatenate([split(v[:, :H], 1), split(v[:, H:], 1)], axis=0) for v in vs]
        vs = [dot(v, xw[...], NN) for v in vs]
        vs = [v[:, :H] + v[:, H:] for v in vs]
        return [jnp.concatenate([v[:H], v[H:]], axis=1) for v in vs]

    def along_y(vs, ws):
        vs = [split(v, 0) for v in vs]
        vs = [dot(w[...], v, NN) for v, w in zip(vs, ws)]
        return [v[:H] + v[H:] for v in vs]

    def step_mid(i, c):
        js = [i * um + k for k in range(um)]
        at = [(j, kind) for j in js for kind in range(2)]
        rows = [pl.ds(pl.multiple_of(j * 16 + 8 * kind, 8), 8) for j, kind in at]
        ws = [(y0, y1)[kind] for _, kind in at]
        vs = [buf[:, r, :].reshape(H, T) for r in rows]
        vs = along_y(along_x(vs), ws)
        ks = [kt[2 * j + kind] for j, kind in at]
        vs = [v * jnp.concatenate([k, k], axis=1) for v, k in zip(vs, ks)]
        vs = along_x(along_y(vs, ws))
        for r, v in zip(rows, vs):
            buf[:, r, :] = v.reshape(n, 8, T)
        return c

    row = lax.broadcasted_iota(jnp.int32, (T, T), 0)
    col = lax.broadcasted_iota(jnp.int32, (T, T), 1)
    eye = (row == col).astype(jnp.float32).astype(jnp.bfloat16)
    fold = (row[:G] == col[:G] % G).astype(jnp.float32).astype(jnp.bfloat16)

    def step_out(i, c):
        ts = [i * uo + k for k in range(uo)]
        phis = [dot(eye, partners(t).reshape(T, T), NT) for t in ts]
        vs = []
        for t in ts:
            v = buf[t].reshape(n, 2, 8, T)
            vs.append((jnp.where(low, v[:, 0], v[:, 1]), zoa))
            vs.append((jnp.where(low, v[:, 1], v[:, 0]), zob))
        vs = [(split(v.reshape(H, T), 0), w) for v, w in vs]
        vs = [dot(w[...], v, NN) for v, w in vs]
        vs = [v[:H] + v[H:] for v in vs]
        vs = [v * phis[k // 2][H * (k % 2) : H * (k % 2) + H] for k, v in enumerate(vs)]
        vs = [split(v[:, :H] + v[:, H:], 1) for v in vs]
        for k, t in enumerate(ts):
            v = dot(fold, jnp.concatenate(vs[2 * k : 2 * k + 2], axis=0), NT)
            out[:, lanes(t)] = v if first else acc[:, lanes(t)] + v
        return c

    lax.fori_loop(0, n // ui, step_in, 0)
    lax.fori_loop(0, n // um, step_mid, 0)
    lax.fori_loop(0, n // uo, step_out, 0)


def pair_terms(own, parts, acc, tabs, kt, steps=(8, 8, 8)):
    vm = pl.BlockSpec(memory_space=pltpu.VMEM)
    first = acc is None
    args = (own, *parts, tabs, kt) + (() if first else (acc,))
    return pl.pallas_call(
        functools.partial(pair_kernel, steps, first),
        out_shape=jax.ShapeDtypeStruct((G, G * G), jnp.float32),
        in_specs=[vm] * len(args),
        out_specs=vm,
        scratch_shapes=[pltpu.VMEM((T // 16, T, T), jnp.float32)],
        compiler_params=pltpu.CompilerParams(vmem_limit_bytes=40 * 1024 * 1024),
        cost_estimate=pl.CostEstimate(flops=13 * 16 * 2 * T**3, bytes_accessed=8 << 20, transcendentals=0),
        name="pair_first" if first else "pair_second",
    )(*args)


def pick_kernel(at, orbitals, low, high, both, own, sems):
    half = 2 * at[0]
    copies = [
        pltpu.make_async_copy(orbitals.at[pl.ds(half, 1)], low, sems.at[0]),
        pltpu.make_async_copy(orbitals.at[pl.ds(half + 1, 1)], high, sems.at[1]),
        pltpu.make_async_copy(orbitals.at[pl.ds(half, 2)], both, sems.at[2]),
        pltpu.make_async_copy(orbitals.at[pl.ds(at[1], 1)], own, sems.at[3]),
    ]
    for copy in copies:
        copy.start()
    for copy in copies:
        copy.wait()


def pick(orbitals, half, mine):
    vm = pl.BlockSpec(memory_space=pltpu.VMEM)
    return pl.pallas_call(
        pick_kernel,
        out_shape=[jax.ShapeDtypeStruct((k, *orbitals.shape[1:]), orbitals.dtype) for k in (1, 1, 2, 1)],
        in_specs=[pl.BlockSpec(memory_space=pltpu.SMEM), pl.BlockSpec(memory_space=pl.ANY)],
        out_specs=[vm] * 4,
        scratch_shapes=[pltpu.SemaphoreType.DMA((4,))],
        compiler_params=pltpu.CompilerParams(vmem_limit_bytes=8 * 1024 * 1024),
        name="pick",
    )(jnp.stack([half, mine]).astype(jnp.int32), orbitals)


def body(orbitals):
    groups, blocks = lax.axis_size("grp"), lax.axis_size("band")
    halves = groups // 2

    def source(g, b, distance):
        s = (b + distance) % blocks
        crosses = b // 4 != s // 4
        return (g ^ 1 if crosses else g) * blocks + s

    def move(v, distances):
        pairs = [(source(g, b, distances[b % 2]), g * blocks + b) for g in range(groups) for b in range(blocks)]
        return lax.ppermute(v, ("grp", "band"), pairs)

    chip, near, far = (1, -1), (-1, 1), (-2, 2)
    group = lax.axis_index("grp")
    low, high, both, own = pick(orbitals, group // halves, group % halves)
    near_low = move(low, near)
    on_chip = move(both, chip)
    near_high = move(high, near)
    near_low, both, kt = lax.optimization_barrier((near_low, both, kernel_table()))
    far_both = move(both, far)
    swapped_low = move(near_low, chip)
    tabs = tables()
    row = pair_terms(own, (on_chip, near_low, swapped_low), None, tabs, kt)
    swapped_high = move(near_high, chip)
    row = pair_terms(own, (far_both, near_high, swapped_high), row, tabs, kt)
    slabs = row.reshape(groups, G // groups, G * G)
    slabs = lax.all_to_all(slabs, "grp", split_axis=0, concat_axis=0, tiled=True)
    return slabs[:halves] + slabs[halves:]


def solution(mesh):
    return jax.shard_map(
        body,
        mesh=mesh,
        in_specs=(P("band", None, None),),
        out_specs=P("band", "grp", None),
        check_vma=False,
    )
```

profile of v0, /device:TPU:1, one launch (start us, length us, event | category | flops | bytes accessed | tf_op | source)
XLA Modules:
  0.0 63.2 jit_solution(2729291179213994247)
XLA Ops:
  0.0 0.1 pad_add_fusion.at
  0.1 0.0 copy-start
  0.1 1.6 %copy-done = bf16[4,64,4096]{2,1,0:T(8,128)(2,1)S(1)} copy-done((bf16[4,64,4096]{2,1,0:T(8,128)(2,1)S(1)}, bf16[4,64,4096]{2,1,0:T(8,128)(2,1)}, u32[]{:S(2)}) %copy-start) | copy-done | bytes 2097176
  1.7 0.0 copy-start.1
  1.7 0.8 %pick.1 = (bf16[1,64,4096]{2,1,0:T(8,128)(2,1)S(1)}, bf16[1,64,4096]{2,1,0:T(8,128)(2,1)S(1)}, bf16[2,64,4096]{2,1,0:T(8,128)(2,1)S(1)}, bf16[1,64,4096]{2,1,0:T(8,128)(2,1)S(1)}) custom-call(s32[2]{0:T(128)S(1)} %pad_add_fusion.at, bf16[4,64,4096]{2,1,0:T(8,128)(2,1)S(1)} %copy-done), custom_call_target="tpu_custom_call" | custom-call | tf_op jit(solution)/shard_map/pick/pallas_call | solution.py:195
  2.4 2.8 %collective-permute-start = (bf16[1,64,4096]{2,1,0:T(8,128)(2,1)S(1)}, bf16[1,64,4096]{2,1,0:T(8,128)(2,1)S(1)}, u32[]{:S(2)}, u32[]{:S(2)}) collective-permute-start(bf16[1,64,4096]{2,1,0:T(8,128)(2,1)S(1)} %get-tuple-element.13), channel_id=1, source_target_pairs={{63,0},{2,1},{1,2},{36,3},{35,4},{6,5},{5,6},{40,7},{39,8},{10,9},... | collective-permute-start | bytes 1572872 | tf_op jit(solution)/shard_map/ppermute | solution.py:217
  5.2 6.6 %collective-permute-start.4 = (bf16[2,64,4096]{2,1,0:T(8,128)(2,1)S(1)}, bf16[2,64,4096]{2,1,0:T(8,128)(2,1)S(1)}, u32[]{:S(2)}, u32[]{:S(2)}) collective-permute-start(bf16[2,64,4096]{2,1,0:T(8,128)(2,1)S(1)} %get-tuple-element.15), channel_id=1, source_target_pairs={{1,0},{0,1},{3,2},{2,3},{5,4},{4,5},{7,6},{6,7},{9,8},{8,9},{11,10... | collective-permute-start | bytes 3145736 | tf_op jit(solution)/shard_map/ppermute | solution.py:217
  11.8 0.0 collective-permute-start.2
  11.9 3.7 %fusion.refs_5_ = f32[32,128,128]{2,1,0:T(8,128)S(1)} fusion(s32[128]{0:T(128)S(1)} %get-tuple-element.25, s32[128]{0:T(128)S(1)} %get-tuple-element.36, s32[32]{0:T(128)S(1)} %get-tuple-element.29, s32[32]{0:T(128)S(1)} %get-tuple-element.33, s32[128]{0:T(128)S(1)} %get-tuple-element.26, s32[128]{0:T(128)S(1)} %get-tuple-element.32, ...), kind=kLoop, calls=%fused_computation.19 | loop fusion | flops 35127296 | bytes 2103488 | tf_op jit(solution)/shard_map/mul | solution.py:63
  15.6 0.0 collective-permute-done.refs_2_
  15.6 3.0 %collective-permute-start.5 = (bf16[1,64,4096]{2,1,0:T(8,128)(2,1)S(1)}, bf16[1,64,4096]{2,1,0:T(8,128)(2,1)S(1)}, u32[]{:S(2)}, u32[]{:S(2)}) collective-permute-start(bf16[1,64,4096]{2,1,0:T(8,128)(2,1)S(1)} %collective-permute-done.refs_2_), channel_id=1, source_target_pairs={{1,0},{0,1},{3,2},{2,3},{5,4},{4,5},{7,6},{6,7},{9,8},{8,9},{11,10... | collective-permute-start | bytes 1572872 | tf_op jit(solution)/shard_map/ppermute | solution.py:217
  18.6 4.7 %collective-permute-start.1 = (bf16[2,64,4096]{2,1,0:T(8,128)(2,1)S(1)}, bf16[2,64,4096]{2,1,0:T(8,128)(2,1)S(1)}, u32[]{:S(2)}, u32[]{:S(2)}) collective-permute-start(bf16[2,64,4096]{2,1,0:T(8,128)(2,1)S(1)} %get-tuple-element.15), channel_id=1, source_target_pairs={{62,0},{3,1},{0,2},{37,3},{34,4},{7,5},{4,6},{41,7},{38,8},{11,9},... | collective-permute-start | bytes 3145736 | tf_op jit(solution)/shard_map/ppermute | solution.py:217
  23.3 0.0 collective-permute-done.2.refs_2_
  23.3 0.9 %collective-permute-start.3 = (bf16[1,64,4096]{2,1,0:T(8,128)(2,1)S(1)}, bf16[1,64,4096]{2,1,0:T(8,128)(2,1)S(1)}, u32[]{:S(2)}, u32[]{:S(2)}) collective-permute-start(bf16[1,64,4096]{2,1,0:T(8,128)(2,1)S(1)} %collective-permute-done.2.refs_2_), channel_id=1, source_target_pairs={{1,0},{0,1},{3,2},{2,3},{5,4},{4,5},{7,6},{6,7},{9,8},{8,9},{11,10... | collective-permute-start | bytes 1572872 | tf_op jit(solution)/shard_map/ppermute | solution.py:217
  24.3 0.0 collective-permute-done.5.refs_3_
  24.3 0.0 collective-permute-done.4.refs_1_
  24.3 0.0 copy-done.1
  24.3 9.3 %pair_first.1.refs_6_ = f32[64,4096]{1,0:T(8,128)S(1)} custom-call(bf16[1,64,4096]{2,1,0:T(8,128)(2,1)S(1)} %get-tuple-element.12.refs_0_, bf16[2,64,4096]{2,1,0:T(8,128)(2,1)S(1)} %collective-permute-done.4.refs_1_, bf16[1,64,4096]{2,1,0:T(8,128)(2,1)S(1)} %collective-permute-done.refs_2_, bf16[1,64,4096]{2,1,0:T(8,128)(2,1)S(1)} %collective-permute-done.5.refs_3_, ...), custom_call_target="tpu_custom_call" | custom-call | flops 6979321856 | bytes 8388608 | tf_op jit(solution)/shard_map/pair_first/pallas_call | solution.py:167
  33.6 0.0 collective-permute-done.3.refs_3_
  33.6 1.4 %collective-permute-done.1.refs_1_ = bf16[2,64,4096]{2,1,0:T(8,128)(2,1)S(1)} collective-permute-done((bf16[2,64,4096]{2,1,0:T(8,128)(2,1)S(1)}, bf16[2,64,4096]{2,1,0:T(8,128)(2,1)S(1)}, u32[]{:S(2)}, u32[]{:S(2)}) %collective-permute-start.1) | collective-permute-done | bytes 1048608 | tf_op jit(solution)/shard_map/ppermute | solution.py:217
  35.0 9.3 %pair_second.1 = f32[64,4096]{1,0:T(8,128)S(1)} custom-call(bf16[1,64,4096]{2,1,0:T(8,128)(2,1)S(1)} %get-tuple-element.12.refs_0_, bf16[2,64,4096]{2,1,0:T(8,128)(2,1)S(1)} %collective-permute-done.1.refs_1_, bf16[1,64,4096]{2,1,0:T(8,128)(2,1)S(1)} %collective-permute-done.2.refs_2_, bf16[1,64,4096]{2,1,0:T(8,128)(2,1)S(1)} %collective-permute-done.3.refs_3_, ...), custom_call_target="tpu_custom_call" | custom-call | flops 6979321856 | bytes 8388608 | tf_op jit(solution)/shard_map/pair_second/pallas_call | solution.py:167
  44.4 18.0 %all_to_all.5 = f32[8,8,4096]{2,1,0:T(8,128)S(1)} all-to-all(f32[8,8,4096]{2,1,0:T(8,128)S(1)} %bitcast.3), channel_id=1, replica_groups=mesh['grp'=8,'band'=32] {'grp'}, dimensions={0} | all-to-all | bytes 2097152 | tf_op jit(solution)/shard_map/all_to_all | solution.py:233
  62.4 0.8 %slice_add_fusion = f32[4,8,4096]{2,1,0:T(8,128)} fusion(f32[8,8,4096]{2,1,0:T(8,128)S(1)} %all_to_all.5), kind=kLoop, calls=%fused_computation.38 | loop fusion | flops 131072 | bytes 1572864 | tf_op jit(solution)/shard_map/add | solution.py:234
  (11 shorter events, 0.1 us)
Async XLA Ops:
  0.1 1.6 %copy-start = (bf16[4,64,4096]{2,1,0:T(8,128)(2,1)S(1)}, bf16[4,64,4096]{2,1,0:T(8,128)(2,1)}, u32[]{:S(2)}) copy-start(bf16[4,64,4096]{2,1,0:T(8,128)(2,1)} %orbitals.1) | copy-start | bytes 6291460
  1.7 22.6 %copy-start.1 = (bf16[7,256,256]{2,1,0:T(8,128)(2,1)S(1)}, bf16[7,256,256]{2,1,0:T(8,128)(2,1)}, u32[]{:S(2)}) copy-start(bf16[7,256,256]{2,1,0:T(8,128)(2,1)} %constant.147.clone.refs_4_) | copy-start | bytes 2752516
  2.4 13.2 %collective-permute-start = (bf16[1,64,4096]{2,1,0:T(8,128)(2,1)S(1)}, bf16[1,64,4096]{2,1,0:T(8,128)(2,1)S(1)}, u32[]{:S(2)}, u32[]{:S(2)}) collective-permute-start(bf16[1,64,4096]{2,1,0:T(8,128)(2,1)S(1)} %get-tuple-element.13), channel_id=1, source_target_pairs={{63,0},{2,1},{1,2},{36,3},{35,4},{6,5},{5,6},{40,7},{39,8},{10,9},... | collective-permute-start | bytes 1572872 | tf_op jit(solution)/shard_map/ppermute | solution.py:217
  5.2 19.1 %collective-permute-start.4 = (bf16[2,64,4096]{2,1,0:T(8,128)(2,1)S(1)}, bf16[2,64,4096]{2,1,0:T(8,128)(2,1)S(1)}, u32[]{:S(2)}, u32[]{:S(2)}) collective-permute-start(bf16[2,64,4096]{2,1,0:T(8,128)(2,1)S(1)} %get-tuple-element.15), channel_id=1, source_target_pairs={{1,0},{0,1},{3,2},{2,3},{5,4},{4,5},{7,6},{6,7},{9,8},{8,9},{11,10... | collective-permute-start | bytes 3145736 | tf_op jit(solution)/shard_map/ppermute | solution.py:217
  11.8 11.5 %collective-permute-start.2 = (bf16[1,64,4096]{2,1,0:T(8,128)(2,1)S(1)}, bf16[1,64,4096]{2,1,0:T(8,128)(2,1)S(1)}, u32[]{:S(2)}, u32[]{:S(2)}) collective-permute-start(bf16[1,64,4096]{2,1,0:T(8,128)(2,1)S(1)} %get-tuple-element.16), channel_id=1, source_target_pairs={{63,0},{2,1},{1,2},{36,3},{35,4},{6,5},{5,6},{40,7},{39,8},{10,9},... | collective-permute-start | bytes 1572872 | tf_op jit(solution)/shard_map/ppermute | solution.py:217
  15.6 8.7 %collective-permute-start.5 = (bf16[1,64,4096]{2,1,0:T(8,128)(2,1)S(1)}, bf16[1,64,4096]{2,1,0:T(8,128)(2,1)S(1)}, u32[]{:S(2)}, u32[]{:S(2)}) collective-permute-start(bf16[1,64,4096]{2,1,0:T(8,128)(2,1)S(1)} %collective-permute-done.refs_2_), channel_id=1, source_target_pairs={{1,0},{0,1},{3,2},{2,3},{5,4},{4,5},{7,6},{6,7},{9,8},{8,9},{11,10... | collective-permute-start | bytes 1572872 | tf_op jit(solution)/shard_map/ppermute | solution.py:217
  18.6 16.4 %collective-permute-start.1 = (bf16[2,64,4096]{2,1,0:T(8,128)(2,1)S(1)}, bf16[2,64,4096]{2,1,0:T(8,128)(2,1)S(1)}, u32[]{:S(2)}, u32[]{:S(2)}) collective-permute-start(bf16[2,64,4096]{2,1,0:T(8,128)(2,1)S(1)} %get-tuple-element.15), channel_id=1, source_target_pairs={{62,0},{3,1},{0,2},{37,3},{34,4},{7,5},{4,6},{41,7},{38,8},{11,9},... | collective-permute-start | bytes 3145736 | tf_op jit(solution)/shard_map/ppermute | solution.py:217
  23.3 10.3 %collective-permute-start.3 = (bf16[1,64,4096]{2,1,0:T(8,128)(2,1)S(1)}, bf16[1,64,4096]{2,1,0:T(8,128)(2,1)S(1)}, u32[]{:S(2)}, u32[]{:S(2)}) collective-permute-start(bf16[1,64,4096]{2,1,0:T(8,128)(2,1)S(1)} %collective-permute-done.2.refs_2_), channel_id=1, source_target_pairs={{1,0},{0,1},{3,2},{2,3},{5,4},{4,5},{7,6},{6,7},{9,8},{8,9},{11,10... | collective-permute-start | bytes 1572872 | tf_op jit(solution)/shard_map/ppermute | solution.py:217
where the time goes:
time: 64.3 us; the launch traced here: 63.2 us
  Pallas kernels  19.4 us (30%)
  starting transfers between devices  18 us (28%)
  blocking collectives  18 us (28%)
  other arithmetic  4.67 us (7%)
  local copies, waits for them, and re-layouts  1.59 us (2%)
  waiting for transfers between devices  1.45 us (2%)
    pallas_call x2, Pallas kernels, pair_terms(): pl.pallas_call(functools.partial(pair_kernel, steps, first), out_shape=ja...  18.7 us
    ppermute x6, starting transfers between devices, move(): return lax.ppermute(v, ('grp', 'band'), pairs)  18 us
    all_to_all x1, blocking collectives, body(): lax.all_to_all(slabs, 'grp', split_axis=0, concat_axis=0, tiled=True)  18 us
    mul x1, other arithmetic, kernel_table(): -0.25 * jnp.where(squared > 0, screened, math.pi / (SCREENING * SCREENING))  3.69 us
    unnamed x4, local copies, waits for them, and re-layouts  1.59 us
    ppermute x6, waiting for transfers between devices, move(): return lax.ppermute(v, ('grp', 'band'), pairs)  1.45 us
  transfers between devices with their start and end apart: 6, of which 1 were waited for; matrix products, arithmetic and copies ran while one was open for 6% of the time, Pallas kernels for 15%

commit v1 on v0

--- a/solution.py
+++ b/solution.py
@@ -152,12 +152,27 @@
         vs = [split(v[:, :H] + v[:, H:], 1) for v in vs]
         for k, t in enumerate(ts):
             v = dot(fold, jnp.concatenate(vs[2 * k : 2 * k + 2], axis=0), NT)
-            out[:, lanes(t)] = v if first else acc[:, lanes(t)] + v
+            if not first:
+                v = acc[:, lanes(t)] + v
+                c = jnp.maximum(c, jnp.maximum(jnp.abs(v[:, :H]), jnp.abs(v[:, H:])))
+            out[:, lanes(t)] = v
         return c
 
     lax.fori_loop(0, n // ui, step_in, 0)
     lax.fori_loop(0, n // um, step_mid, 0)
-    lax.fori_loop(0, n // uo, step_out, 0)
+    largest = lax.fori_loop(0, n // uo, step_out, jnp.zeros((G, H), jnp.float32))
+    if not first:
+        power = jnp.full((G, H), jnp.clip(jnp.max(largest), 1e-30, 1e30), jnp.float32)
+        power = jnp.round(jnp.log2(power))
+        scale = jnp.tile(jnp.exp2(-power), (1, T // H))
+        out[:, G * G :] = power
+
+        def step_code(t, c):
+            v = out[:, lanes(t)] * scale
+            out[:, lanes(t)] = v * jnp.abs(v) * 4096.0
+            return c
+
+        lax.fori_loop(0, n, step_code, 0, unroll=4)
 
 
 def pair_terms(own, parts, acc, tabs, kt, steps=(8, 8, 8)):
@@ -166,7 +181,7 @@
     args = (own, *parts, tabs, kt) + (() if first else (acc,))
     return pl.pallas_call(
         functools.partial(pair_kernel, steps, first),
-        out_shape=jax.ShapeDtypeStruct((G, G * G), jnp.float32),
+        out_shape=jax.ShapeDtypeStruct((G, G * G + (0 if first else H)), jnp.float32),
         in_specs=[vm] * len(args),
         out_specs=vm,
         scratch_shapes=[pltpu.VMEM((T // 16, T, T), jnp.float32)],
@@ -195,12 +210,18 @@
     return pl.pallas_call(
         pick_kernel,
         out_shape=[jax.ShapeDtypeStruct((k, *orbitals.shape[1:]), orbitals.dtype) for k in (1, 1, 2, 1)],
-        in_specs=[pl.BlockSpec(memory_space=pltpu.SMEM), pl.BlockSpec(memory_space=pl.ANY)],
+        in_specs=[pl.BlockSpec(memory_space=pltpu.SMEM), pl.BlockSpec(memory_space=pltpu.HBM)],
         out_specs=[vm] * 4,
         scratch_shapes=[pltpu.SemaphoreType.DMA((4,))],
         compiler_params=pltpu.CompilerParams(vmem_limit_bytes=8 * 1024 * 1024),
         name="pick",
     )(jnp.stack([half, mine]).astype(jnp.int32), orbitals)
+
+
+def decoded(slabs, power):
+    v = slabs.astype(jnp.float32)
+    root = jnp.sqrt(jnp.abs(v)) * power
+    return jnp.where(v < 0, -root, root)
 
 
 def body(orbitals):
@@ -222,16 +243,19 @@
     near_low = move(low, near)
     on_chip = move(both, chip)
     near_high = move(high, near)
-    near_low, both, kt = lax.optimization_barrier((near_low, both, kernel_table()))
+    kt = kernel_table()
+    near_low, kt = lax.optimization_barrier((near_low, kt))
     far_both = move(both, far)
     swapped_low = move(near_low, chip)
     tabs = tables()
     row = pair_terms(own, (on_chip, near_low, swapped_low), None, tabs, kt)
     swapped_high = move(near_high, chip)
     row = pair_terms(own, (far_both, near_high, swapped_high), row, tabs, kt)
-    slabs = row.reshape(groups, G // groups, G * G)
+    slabs = row.astype(jnp.float16).reshape(groups, G // groups, -1)
     slabs = lax.all_to_all(slabs, "grp", split_axis=0, concat_axis=0, tiled=True)
-    return slabs[:halves] + slabs[halves:]
+    slabs, power = slabs[..., : G * G], slabs[:, :1, G * G : G * G + 1]
+    power = jnp.exp2(power.astype(jnp.float32)) * (1.0 / 64.0)
+    return decoded(slabs[:halves], power[:halves]) + decoded(slabs[halves:], power[halves:])
 
 
 def solution(mesh):

time: 64.3 us -> 60.7 us (0.944)
  blocking collectives: 18 us -> 13.7 us
    all_to_all x1, blocking collectives: 18 us -> 13.7 us  [body(): lax.all_to_all(slabs, 'grp', split_axis=0, concat_axis=0, tiled=True)]
  transfers between devices with their start and end apart: 6 -> 6, of which waited for: 1 -> 1; matrix products, arithmetic and copies ran while one was open for 6% -> 6% of each run, Pallas kernels for 15% -> 16%
where the time goes in v1:
time: 60.7 us; the launch traced here: 60 us
  Pallas kernels  19.8 us (33%)
  starting transfers between devices  18 us (30%)
  blocking collectives  13.7 us (23%)
  other arithmetic  5.17 us (9%)
  local copies, waits for them, and re-layouts  1.75 us (3%)
  waiting for transfers between devices  1.45 us (2%)
    pallas_call x2, Pallas kernels, pair_terms(): pl.pallas_call(functools.partial(pair_kernel, steps, first), out_shape=ja...  19 us
    ppermute x6, starting transfers between devices, move(): return lax.ppermute(v, ('grp', 'band'), pairs)  18 us
    all_to_all x1, blocking collectives, body(): lax.all_to_all(slabs, 'grp', split_axis=0, concat_axis=0, tiled=True)  13.7 us
    mul x1, other arithmetic, kernel_table(): -0.25 * jnp.where(squared > 0, screened, math.pi / (SCREENING * SCREENING))  3.69 us
    unnamed x4, local copies, waits for them, and re-layouts  1.59 us
    ppermute x6, waiting for transfers between devices, move(): return lax.ppermute(v, ('grp', 'band'), pairs)  1.45 us
    add x1, other arithmetic, body(): decoded(slabs[:halves], power[:halves])  1.28 us
  transfers between devices with their start and end apart: 6, of which 1 were waited for; matrix products, arithmetic and copies ran while one was open for 6% of the time, Pallas kernels for 16%

profile of v1, /device:TPU:1, one launch (start us, length us, event | category | flops | bytes accessed | tf_op | source)
XLA Modules:
  0.0 60.0 jit_solution(5357274645139699459)
XLA Ops:
  0.0 0.1 pad_add_fusion.at
  0.1 0.0 copy-start
  0.1 1.6 %copy-done = bf16[4,64,4096]{2,1,0:T(8,128)(2,1)S(1)} copy-done((bf16[4,64,4096]{2,1,0:T(8,128)(2,1)S(1)}, bf16[4,64,4096]{2,1,0:T(8,128)(2,1)}, u32[]{:S(2)}) %copy-start) | copy-done | bytes 2097176
  1.7 0.0 copy-start.1
  1.7 0.8 %pick.1 = (bf16[1,64,4096]{2,1,0:T(8,128)(2,1)S(1)}, bf16[1,64,4096]{2,1,0:T(8,128)(2,1)S(1)}, bf16[2,64,4096]{2,1,0:T(8,128)(2,1)S(1)}, bf16[1,64,4096]{2,1,0:T(8,128)(2,1)S(1)}) custom-call(s32[2]{0:T(128)S(1)} %pad_add_fusion.at, bf16[4,64,4096]{2,1,0:T(8,128)(2,1)S(1)} %copy-done), custom_call_target="tpu_custom_call" | custom-call | tf_op jit(solution)/shard_map/pick/pallas_call | solution.py:210
  2.4 2.8 %collective-permute-start.3 = (bf16[1,64,4096]{2,1,0:T(8,128)(2,1)S(1)}, bf16[1,64,4096]{2,1,0:T(8,128)(2,1)S(1)}, u32[]{:S(2)}, u32[]{:S(2)}) collective-permute-start(bf16[1,64,4096]{2,1,0:T(8,128)(2,1)S(1)} %get-tuple-element.14), channel_id=1, source_target_pairs={{63,0},{2,1},{1,2},{36,3},{35,4},{6,5},{5,6},{40,7},{39,8},{10,9},... | collective-permute-start | bytes 1572872 | tf_op jit(solution)/shard_map/ppermute | solution.py:238
  5.2 6.6 %collective-permute-start.4 = (bf16[2,64,4096]{2,1,0:T(8,128)(2,1)S(1)}, bf16[2,64,4096]{2,1,0:T(8,128)(2,1)S(1)}, u32[]{:S(2)}, u32[]{:S(2)}) collective-permute-start(bf16[2,64,4096]{2,1,0:T(8,128)(2,1)S(1)} %get-tuple-element.12), channel_id=1, source_target_pairs={{1,0},{0,1},{3,2},{2,3},{5,4},{4,5},{7,6},{6,7},{9,8},{8,9},{11,10... | collective-permute-start | bytes 3145736 | tf_op jit(solution)/shard_map/ppermute | solution.py:238
  11.8 0.0 collective-permute-start.1
  11.9 3.7 %fusion.refs_5_ = f32[32,128,128]{2,1,0:T(8,128)S(1)} fusion(s32[128]{0:T(128)S(1)} %get-tuple-element.25, s32[128]{0:T(128)S(1)} %get-tuple-element.36, s32[32]{0:T(128)S(1)} %get-tuple-element.29, s32[32]{0:T(128)S(1)} %get-tuple-element.33, s32[128]{0:T(128)S(1)} %get-tuple-element.26, s32[128]{0:T(128)S(1)} %get-tuple-element.32, ...), kind=kLoop, calls=%fused_computation.19 | loop fusion | flops 35127296 | bytes 2103488 | tf_op jit(solution)/shard_map/mul | solution.py:63
  15.6 0.0 collective-permute-done.3.refs_2_
  15.6 3.0 %collective-permute-start.5 = (bf16[1,64,4096]{2,1,0:T(8,128)(2,1)S(1)}, bf16[1,64,4096]{2,1,0:T(8,128)(2,1)S(1)}, u32[]{:S(2)}, u32[]{:S(2)}) collective-permute-start(bf16[1,64,4096]{2,1,0:T(8,128)(2,1)S(1)} %collective-permute-done.3.refs_2_), channel_id=1, source_target_pairs={{1,0},{0,1},{3,2},{2,3},{5,4},{4,5},{7,6},{6,7},{9,8},{8,9},{11,10... | collective-permute-start | bytes 1572872 | tf_op jit(solution)/shard_map/ppermute | solution.py:238
  18.6 4.7 %collective-permute-start = (bf16[2,64,4096]{2,1,0:T(8,128)(2,1)S(1)}, bf16[2,64,4096]{2,1,0:T(8,128)(2,1)S(1)}, u32[]{:S(2)}, u32[]{:S(2)}) collective-permute-start(bf16[2,64,4096]{2,1,0:T(8,128)(2,1)S(1)} %get-tuple-element.12), channel_id=1, source_target_pairs={{62,0},{3,1},{0,2},{37,3},{34,4},{7,5},{4,6},{41,7},{38,8},{11,9},... | collective-permute-start | bytes 3145736 | tf_op jit(solution)/shard_map/ppermute | solution.py:238
  23.3 0.0 collective-permute-done.1.refs_2_
  23.3 0.9 %collective-permute-start.2 = (bf16[1,64,4096]{2,1,0:T(8,128)(2,1)S(1)}, bf16[1,64,4096]{2,1,0:T(8,128)(2,1)S(1)}, u32[]{:S(2)}, u32[]{:S(2)}) collective-permute-start(bf16[1,64,4096]{2,1,0:T(8,128)(2,1)S(1)} %collective-permute-done.1.refs_2_), channel_id=1, source_target_pairs={{1,0},{0,1},{3,2},{2,3},{5,4},{4,5},{7,6},{6,7},{9,8},{8,9},{11,10... | collective-permute-start | bytes 1572872 | tf_op jit(solution)/shard_map/ppermute | solution.py:238
  24.3 0.0 collective-permute-done.5.refs_3_
  24.3 0.0 collective-permute-done.4.refs_1_
  24.3 0.0 copy-done.1
  24.3 9.3 %pair_first.1.refs_6_ = f32[64,4096]{1,0:T(8,128)S(1)} custom-call(bf16[1,64,4096]{2,1,0:T(8,128)(2,1)S(1)} %get-tuple-element.11.refs_0_, bf16[2,64,4096]{2,1,0:T(8,128)(2,1)S(1)} %collective-permute-done.4.refs_1_, bf16[1,64,4096]{2,1,0:T(8,128)(2,1)S(1)} %collective-permute-done.3.refs_2_, bf16[1,64,4096]{2,1,0:T(8,128)(2,1)S(1)} %collective-permute-done.5.refs_3_, ...), custom_call_target="tpu_custom_call" | custom-call | flops 6979321856 | bytes 8388608 | tf_op jit(solution)/shard_map/pair_first/pallas_call | solution.py:182
  33.6 0.0 collective-permute-done.2.refs_3_
  33.6 1.4 %collective-permute-done.refs_1_ = bf16[2,64,4096]{2,1,0:T(8,128)(2,1)S(1)} collective-permute-done((bf16[2,64,4096]{2,1,0:T(8,128)(2,1)S(1)}, bf16[2,64,4096]{2,1,0:T(8,128)(2,1)S(1)}, u32[]{:S(2)}, u32[]{:S(2)}) %collective-permute-start) | collective-permute-done | bytes 1048608 | tf_op jit(solution)/shard_map/ppermute | solution.py:238
  35.0 9.7 %pair_second.1 = f32[64,4224]{1,0:T(8,128)S(1)} custom-call(bf16[1,64,4096]{2,1,0:T(8,128)(2,1)S(1)} %get-tuple-element.11.refs_0_, bf16[2,64,4096]{2,1,0:T(8,128)(2,1)S(1)} %collective-permute-done.refs_1_, bf16[1,64,4096]{2,1,0:T(8,128)(2,1)S(1)} %collective-permute-done.1.refs_2_, bf16[1,64,4096]{2,1,0:T(8,128)(2,1)S(1)} %collective-permute-done.2.refs_3_, ...), custom_call_target="tpu_custom_call" | custom-call | flops 6979321856 | bytes 8388608 | tf_op jit(solution)/shard_map/pair_second/pallas_call | solution.py:182
  44.7 0.1 convert_bitcast_fusion
  44.8 13.7 %all_to_all.5 = f16[8,8,4224]{2,1,0:T(8,128)(2,1)S(1)} all-to-all(f16[8,8,4224]{2,1,0:T(8,128)(2,1)S(1)} %convert_bitcast_fusion), channel_id=1, replica_groups=mesh['grp'=8,'band'=32] {'grp'}, dimensions={0} | all-to-all | bytes 1081344 | tf_op jit(solution)/shard_map/all_to_all | solution.py:255
  58.6 0.2 slice_reduce_fusion.1
  58.7 1.3 %fusion.23 = f32[4,8,4096]{2,1,0:T(8,128)} fusion(f16[8,8,4224]{2,1,0:T(8,128)(2,1)S(1)} %all_to_all.5, f32[4]{0:T(128)S(1)} %get-tuple-element.18, f32[4]{0:T(128)S(1)} %get-tuple-element.17), kind=kLoop, calls=%fused_computation.49 | loop fusion | flops 1703936 | bytes 1048608 | tf_op jit(solution)/shard_map/add | solution.py:258
  (13 shorter events, 0.1 us)
Async XLA Ops:
  0.1 1.6 %copy-start = (bf16[4,64,4096]{2,1,0:T(8,128)(2,1)S(1)}, bf16[4,64,4096]{2,1,0:T(8,128)(2,1)}, u32[]{:S(2)}) copy-start(bf16[4,64,4096]{2,1,0:T(8,128)(2,1)} %orbitals.1) | copy-start | bytes 6291460
  1.7 22.6 %copy-start.1 = (bf16[7,256,256]{2,1,0:T(8,128)(2,1)S(1)}, bf16[7,256,256]{2,1,0:T(8,128)(2,1)}, u32[]{:S(2)}) copy-start(bf16[7,256,256]{2,1,0:T(8,128)(2,1)} %constant.152.clone.refs_4_) | copy-start | bytes 2752516
  2.4 13.2 %collective-permute-start.3 = (bf16[1,64,4096]{2,1,0:T(8,128)(2,1)S(1)}, bf16[1,64,4096]{2,1,0:T(8,128)(2,1)S(1)}, u32[]{:S(2)}, u32[]{:S(2)}) collective-permute-start(bf16[1,64,4096]{2,1,0:T(8,128)(2,1)S(1)} %get-tuple-element.14), channel_id=1, source_target_pairs={{63,0},{2,1},{1,2},{36,3},{35,4},{6,5},{5,6},{40,7},{39,8},{10,9},... | collective-permute-start | bytes 1572872 | tf_op jit(solution)/shard_map/ppermute | solution.py:238
  5.2 19.1 %collective-permute-start.4 = (bf16[2,64,4096]{2,1,0:T(8,128)(2,1)S(1)}, bf16[2,64,4096]{2,1,0:T(8,128)(2,1)S(1)}, u32[]{:S(2)}, u32[]{:S(2)}) collective-permute-start(bf16[2,64,4096]{2,1,0:T(8,128)(2,1)S(1)} %get-tuple-element.12), channel_id=1, source_target_pairs={{1,0},{0,1},{3,2},{2,3},{5,4},{4,5},{7,6},{6,7},{9,8},{8,9},{11,10... | collective-permute-start | bytes 3145736 | tf_op jit(solution)/shard_map/ppermute | solution.py:238
  11.8 11.5 %collective-permute-start.1 = (bf16[1,64,4096]{2,1,0:T(8,128)(2,1)S(1)}, bf16[1,64,4096]{2,1,0:T(8,128)(2,1)S(1)}, u32[]{:S(2)}, u32[]{:S(2)}) collective-permute-start(bf16[1,64,4096]{2,1,0:T(8,128)(2,1)S(1)} %get-tuple-element.13), channel_id=1, source_target_pairs={{63,0},{2,1},{1,2},{36,3},{35,4},{6,5},{5,6},{40,7},{39,8},{10,9},... | collective-permute-start | bytes 1572872 | tf_op jit(solution)/shard_map/ppermute | solution.py:238
  15.6 8.7 %collective-permute-start.5 = (bf16[1,64,4096]{2,1,0:T(8,128)(2,1)S(1)}, bf16[1,64,4096]{2,1,0:T(8,128)(2,1)S(1)}, u32[]{:S(2)}, u32[]{:S(2)}) collective-permute-start(bf16[1,64,4096]{2,1,0:T(8,128)(2,1)S(1)} %collective-permute-done.3.refs_2_), channel_id=1, source_target_pairs={{1,0},{0,1},{3,2},{2,3},{5,4},{4,5},{7,6},{6,7},{9,8},{8,9},{11,10... | collective-permute-start | bytes 1572872 | tf_op jit(solution)/shard_map/ppermute | solution.py:238
  18.6 16.4 %collective-permute-start = (bf16[2,64,4096]{2,1,0:T(8,128)(2,1)S(1)}, bf16[2,64,4096]{2,1,0:T(8,128)(2,1)S(1)}, u32[]{:S(2)}, u32[]{:S(2)}) collective-permute-start(bf16[2,64,4096]{2,1,0:T(8,128)(2,1)S(1)} %get-tuple-element.12), channel_id=1, source_target_pairs={{62,0},{3,1},{0,2},{37,3},{34,4},{7,5},{4,6},{41,7},{38,8},{11,9},... | collective-permute-start | bytes 3145736 | tf_op jit(solution)/shard_map/ppermute | solution.py:238
  23.3 10.3 %collective-permute-start.2 = (bf16[1,64,4096]{2,1,0:T(8,128)(2,1)S(1)}, bf16[1,64,4096]{2,1,0:T(8,128)(2,1)S(1)}, u32[]{:S(2)}, u32[]{:S(2)}) collective-permute-start(bf16[1,64,4096]{2,1,0:T(8,128)(2,1)S(1)} %collective-permute-done.1.refs_2_), channel_id=1, source_target_pairs={{1,0},{0,1},{3,2},{2,3},{5,4},{4,5},{7,6},{6,7},{9,8},{8,9},{11,10... | collective-permute-start | bytes 1572872 | tf_op jit(solution)/shard_map/ppermute | solution.py:238

commit v2 on v0

--- a/solution.py
+++ b/solution.py
@@ -15,6 +15,8 @@
 G = 64
 H = 128
 T = 256
+CODE_SHIFT = 118
+CUTS = 2
 
 
 def split_table(m):
@@ -77,11 +79,20 @@
     return jnp.concatenate([hi, lo], axis=axis)
 
 
-def pair_kernel(steps, first, *refs):
+def pair_kernel(steps, own_hbm, pa_hbm, pb_hbm, pc_hbm, pd_hbm, tabs_hbm, kt_hbm, out, *scratch):
     ui, um, uo = steps
-    own, pa, pb, pc, tabs, kt = refs[:6]
-    acc = None if first else refs[6]
-    out, buf = refs[-2:]
+    own, pa, pb, pc, pd, tabs, kt, buf, row_buf, sems = scratch
+    tabs_copy = pltpu.make_async_copy(tabs_hbm, tabs, sems.at[0])
+    kt_copy = pltpu.make_async_copy(kt_hbm, kt, sems.at[1])
+    size = G * G // CUTS
+    band_copies = []
+    for c in range(CUTS):
+        at = pl.ds(c * size, size)
+        for k, (a, b) in enumerate(((own_hbm, own), (pa_hbm, pa), (pb_hbm, pb), (pc_hbm, pc), (pd_hbm, pd))):
+            band_copies.append(pltpu.make_async_copy(a.at[:, :, at], b.at[:, :, at], sems.at[2 + 5 * c + k]))
+    for copy in (tabs_copy, *band_copies, kt_copy):
+        copy.start()
+    tabs_copy.wait()
     zia, zoa, zib, zob, y0, y1, xw = (tabs.at[k] for k in range(7))
     n = T // 16
     low = lax.broadcasted_iota(jnp.int32, (n, 8, T), 1) < 4
@@ -90,7 +101,7 @@
         return pl.ds(pl.multiple_of(t * size, size), size)
 
     def partners(t, size=T):
-        return jnp.concatenate([p[:, :, lanes(t, size)] for p in (pa, pb, pc)], axis=0)
+        return jnp.concatenate([p[:, :, lanes(t, size)] for p in (pa, pb, pc, pd)], axis=0)
 
     def step_in(i, c):
         ts = [i * ui + k for k in range(ui)]
@@ -152,60 +163,95 @@
         vs = [split(v[:, :H] + v[:, H:], 1) for v in vs]
         for k, t in enumerate(ts):
             v = dot(fold, jnp.concatenate(vs[2 * k : 2 * k + 2], axis=0), NT)
-            out[:, lanes(t)] = v if first else acc[:, lanes(t)] + v
-        return c
-
-    lax.fori_loop(0, n // ui, step_in, 0)
+            c = jnp.maximum(c, jnp.maximum(jnp.abs(v[:, :H]), jnp.abs(v[:, H:])))
+            row_buf[:, lanes(t)] = v
+        return c
+
+    for c in range(CUTS):
+        for copy in band_copies[5 * c : 5 * c + 5]:
+            copy.wait()
+        lax.fori_loop(c * n // ui // CUTS, (c + 1) * n // ui // CUTS, step_in, 0)
+    kt_copy.wait()
     lax.fori_loop(0, n // um, step_mid, 0)
-    lax.fori_loop(0, n // uo, step_out, 0)
-
-
-def pair_terms(own, parts, acc, tabs, kt, steps=(8, 8, 8)):
+    largest = lax.fori_loop(0, n // uo, step_out, jnp.zeros((G, H), jnp.float32))
+    power = jnp.full((G, H), jnp.clip(jnp.max(largest), 1e-30, 1e30), jnp.float32)
+    power = jnp.round(jnp.log2(power))
+    scale = jnp.tile(jnp.exp2(-power), (1, T // H))
+    out[:, G * G :] = power.astype(out.dtype)
+
+    def step_code(t, c):
+        v = row_buf[:, lanes(t)] * scale
+        r = v * v
+        r = r * r
+        r = r * r * 2.0 ** (CODE_SHIFT // 2)
+        r = r * r
+        out[:, lanes(t)] = jnp.where(v < 0, -r, r).astype(out.dtype)
+        return c
+
+    lax.fori_loop(0, n, step_code, 0, unroll=4)
+
+
+def pair_row(own, parts, tabs, kt, limit_mib, steps=(8, 8, 8)):
+    args = (own, *parts, tabs, kt)
+    return pl.pallas_call(
+        functools.partial(pair_kernel, steps),
+        out_shape=jax.ShapeDtypeStruct((G, G * G + H), jnp.bfloat16),
+        in_specs=[pl.BlockSpec(memory_space=pl.ANY)] * len(args),
+        out_specs=pl.BlockSpec(memory_space=pltpu.VMEM),
+        scratch_shapes=[
+            *(pltpu.VMEM(v.shape, v.dtype) for v in args),
+            pltpu.VMEM((T // 16, T, T), jnp.float32),
+            pltpu.VMEM((G, G * G), jnp.float32),
+            pltpu.SemaphoreType.DMA((2 + 5 * CUTS,)),
+        ],
+        compiler_params=pltpu.CompilerParams(vmem_limit_bytes=limit_mib * 1024 * 1024),
+        cost_estimate=pl.CostEstimate(flops=13 * 16 * 2 * T**3, bytes_accessed=8 << 20, transcendentals=0),
+        name="pair_row",
+    )(*args)
+
+
+def gather_kernel(count, *refs):
+    *earlier, slabs, out = refs
+    first = 0
+    for ref in earlier:
+        out[: ref.shape[0]] = ref[...]
+        first += ref.shape[0]
+    size = slabs.shape[-1] - H
+    wide = 4 * H
+
+    def step(t, c):
+        at = pl.ds(pl.multiple_of(t * wide, wide), wide)
+        for k in range(count):
+            total = None
+            for s in range(k, slabs.shape[0], count):
+                v = slabs[s, :, at].astype(jnp.float32)
+                power = slabs[s, :, size:].astype(jnp.float32) - CODE_SHIFT / 16
+                v_root = jnp.exp2(jnp.log2(jnp.abs(v)) * (1 / 16) + jnp.tile(power, (1, wide // H)))
+                v = jnp.where(v == 0, 0.0, jnp.where(v < 0, -v_root, v_root))
+                total = v if total is None else total + v
+            out[first + k, :, at] = total
+        return c
+
+    lax.fori_loop(0, size // wide, step, 0, unroll=2)
+
+
+def gathered(slabs, count, earlier=()):
     vm = pl.BlockSpec(memory_space=pltpu.VMEM)
-    first = acc is None
-    args = (own, *parts, tabs, kt) + (() if first else (acc,))
+    rows = count + sum(v.shape[0] for v in earlier)
     return pl.pallas_call(
-        functools.partial(pair_kernel, steps, first),
-        out_shape=jax.ShapeDtypeStruct((G, G * G), jnp.float32),
-        in_specs=[vm] * len(args),
+        functools.partial(gather_kernel, count),
+        out_shape=jax.ShapeDtypeStruct((rows, slabs.shape[1], slabs.shape[2] - H), jnp.float32),
+        in_specs=[vm] * (1 + len(earlier)),
         out_specs=vm,
-        scratch_shapes=[pltpu.VMEM((T // 16, T, T), jnp.float32)],
-        compiler_params=pltpu.CompilerParams(vmem_limit_bytes=40 * 1024 * 1024),
-        cost_estimate=pl.CostEstimate(flops=13 * 16 * 2 * T**3, bytes_accessed=8 << 20, transcendentals=0),
-        name="pair_first" if first else "pair_second",
-    )(*args)
-
-
-def pick_kernel(at, orbitals, low, high, both, own, sems):
-    half = 2 * at[0]
-    copies = [
-        pltpu.make_async_copy(orbitals.at[pl.ds(half, 1)], low, sems.at[0]),
-        pltpu.make_async_copy(orbitals.at[pl.ds(half + 1, 1)], high, sems.at[1]),
-        pltpu.make_async_copy(orbitals.at[pl.ds(half, 2)], both, sems.at[2]),
-        pltpu.make_async_copy(orbitals.at[pl.ds(at[1], 1)], own, sems.at[3]),
-    ]
-    for copy in copies:
-        copy.start()
-    for copy in copies:
-        copy.wait()
-
-
-def pick(orbitals, half, mine):
-    vm = pl.BlockSpec(memory_space=pltpu.VMEM)
-    return pl.pallas_call(
-        pick_kernel,
-        out_shape=[jax.ShapeDtypeStruct((k, *orbitals.shape[1:]), orbitals.dtype) for k in (1, 1, 2, 1)],
-        in_specs=[pl.BlockSpec(memory_space=pltpu.SMEM), pl.BlockSpec(memory_space=pl.ANY)],
-        out_specs=[vm] * 4,
-        scratch_shapes=[pltpu.SemaphoreType.DMA((4,))],
-        compiler_params=pltpu.CompilerParams(vmem_limit_bytes=8 * 1024 * 1024),
-        name="pick",
-    )(jnp.stack([half, mine]).astype(jnp.int32), orbitals)
+        compiler_params=pltpu.CompilerParams(vmem_limit_bytes=16 * 1024 * 1024),
+        cost_estimate=pl.CostEstimate(flops=1 << 22, bytes_accessed=1 << 20, transcendentals=1 << 19),
+        name="gathered",
+    )(*earlier, slabs)
 
 
 def body(orbitals):
     groups, blocks = lax.axis_size("grp"), lax.axis_size("band")
-    halves = groups // 2
+    halves = groups // 4
 
     def source(g, b, distance):
         s = (b + distance) % blocks
@@ -216,22 +262,27 @@
         pairs = [(source(g, b, distances[b % 2]), g * blocks + b) for g in range(groups) for b in range(blocks)]
         return lax.ppermute(v, ("grp", "band"), pairs)
 
+    def spread(row):
+        slabs = row.reshape(groups, G // groups, -1)
+        return lax.all_to_all(slabs, "grp", split_axis=0, concat_axis=0, tiled=True)
+
     chip, near, far = (1, -1), (-1, 1), (-2, 2)
     group = lax.axis_index("grp")
-    low, high, both, own = pick(orbitals, group // halves, group % halves)
-    near_low = move(low, near)
-    on_chip = move(both, chip)
-    near_high = move(high, near)
-    near_low, both, kt = lax.optimization_barrier((near_low, both, kernel_table()))
-    far_both = move(both, far)
-    swapped_low = move(near_low, chip)
+    mine = lax.dynamic_slice_in_dim(orbitals, group // halves, 1, 0)
+    from_near = move(mine, near)
+    from_chip = move(mine, chip)
+    kt = kernel_table()
+    from_far = move(mine, far)
+    swapped = move(from_near, chip)
+    parts = (from_chip, from_near, swapped, from_far)
     tabs = tables()
-    row = pair_terms(own, (on_chip, near_low, swapped_low), None, tabs, kt)
-    swapped_high = move(near_high, chip)
-    row = pair_terms(own, (far_both, near_high, swapped_high), row, tabs, kt)
-    slabs = row.reshape(groups, G // groups, G * G)
-    slabs = lax.all_to_all(slabs, "grp", split_axis=0, concat_axis=0, tiled=True)
-    return slabs[:halves] + slabs[halves:]
+    owns = [lax.dynamic_slice_in_dim(orbitals, group % halves + k, 1, 0) for k in range(0, 2 * halves, halves)]
+    row = pair_row(owns[0], parts, tabs, kt, 40)
+    slabs = spread(row)
+    low = gathered(slabs, halves)
+    row = pair_row(owns[1], parts, tabs, kt, 62)
+    slabs = spread(row)
+    return gathered(slabs, halves, (low,))
 
 
 def solution(mesh):

time: 64.3 us -> 74.3 us (1.16); the launches traced: 63.2 us -> 74.1 us
  blocking collectives: 18 us -> 0 us
  waiting for transfers between devices: 1.45 us -> 18.2 us
  starting transfers between devices: 18 us -> 24.4 us
  Pallas kernels: 19.4 us -> 25.1 us
  other arithmetic: 4.67 us -> 3.74 us
  local copies, waits for them, and re-layouts: 1.59 us -> 2.41 us
    all_to_all x1 -> x0, blocking collectives: 18 us -> none  [body(): lax.all_to_all(slabs, 'grp', split_axis=0, concat_axis=0, tiled=True)]
    all_to_all x0 -> x2, starting transfers between devices: none -> 10.7 us  [spread(): return lax.all_to_all(slabs, 'grp', split_axis=0, concat_axis=0, tiled=True)]
    all_to_all x0 -> x2, waiting for transfers between devices: none -> 10.3 us  [spread(): return lax.all_to_all(slabs, 'grp', split_axis=0, concat_axis=0, tiled=True)]
    ppermute x6 -> x4, waiting for transfers between devices: 1.45 us -> 7.94 us  [move(): return lax.ppermute(v, ('grp', 'band'), pairs)]
    pallas_call x3 -> x4, Pallas kernels: 19.4 us -> 25.1 us  [the longest x2 23.4 us: pair_row(): pl.pallas_call(functools.partial(pair_kernel, steps), out_shape=jax.Shape...]
    ppermute x6 -> x4, starting transfers between devices: 18 us -> 13.7 us  [move(): return lax.ppermute(v, ('grp', 'band'), pairs)]
    dynamic_slice x0 -> x1, local copies, waits for them, and re-layouts: none -> 2.38 us  [body(): lax.dynamic_slice_in_dim(orbitals, group % halves + k, 1, 0)]
    unnamed x4 -> x12, local copies, waits for them, and re-layouts: 1.59 us -> 0.02 us
  transfers between devices with their start and end apart: 6 -> 6, of which waited for: 1 -> 2; matrix products, arithmetic and copies ran while one was open for 6% -> 5% of each run, Pallas kernels for 15% -> 17%
where the time goes in v2:
time: 74.3 us; the launch traced here: 74.1 us
  Pallas kernels  25.1 us (34%)
  starting transfers between devices  24.4 us (33%)
  waiting for transfers between devices  18.2 us (24%)
  other arithmetic  3.74 us (5%)
  local copies, waits for them, and re-layouts  2.41 us (3%)
    pallas_call x2, Pallas kernels, pair_row(): pl.pallas_call(functools.partial(pair_kernel, steps), out_shape=jax.Shape...  23.4 us
    ppermute x4, starting transfers between devices, move(): return lax.ppermute(v, ('grp', 'band'), pairs)  13.7 us
    all_to_all x2, starting transfers between devices, spread(): return lax.all_to_all(slabs, 'grp', split_axis=0, concat_axis=0, tiled=True)  10.7 us
    all_to_all x2, waiting for transfers between devices, spread(): return lax.all_to_all(slabs, 'grp', split_axis=0, concat_axis=0, tiled=True)  10.3 us
    ppermute x4, waiting for transfers between devices, move(): return lax.ppermute(v, ('grp', 'band'), pairs)  7.94 us
    mul x1, other arithmetic, kernel_table(): -0.25 * jnp.where(squared > 0, screened, math.pi / (SCREENING * SCREENING))  3.69 us
    dynamic_slice x1, local copies, waits for them, and re-layouts, body(): lax.dynamic_slice_in_dim(orbitals, group % halves + k, 1, 0)  2.38 us
    pallas_call x2, Pallas kernels, gathered(): pl.pallas_call(functools.partial(gather_kernel, count), out_shape=jax.Sha...  1.7 us
  transfers between devices with their start and end apart: 6, of which 2 were waited for; matrix products, arithmetic and copies ran while one was open for 5% of the time, Pallas kernels for 17%

profile of v2, /device:TPU:1, one launch (start us, length us, event | category | flops | bytes accessed | tf_op | source)
XLA Modules:
  0.0 74.1 jit_solution(17839328985676435426)
XLA Ops:
  0.0 0.0 copy-start.5
  0.0 2.4 %constant_dynamic-slice_fusion = (bf16[1,64,4096]{2,1,0:T(8,128)(2,1)}, bf16[1,64,4096]{2,1,0:T(8,128)(2,1)S(1)}, bf16[1,64,4096]{2,1,0:T(8,128)(2,1)S(1)}) fusion(bf16[4,64,4096]{2,1,0:T(8,128)(2,1)} %param.2, s32[]{:T(128)S(6)} %select_n.120, s32[]{:T(128)S(6)} %select_n.103, s32[]{:T(128)S(6)} %select_n.105), kind=kLoop, calls=%fused_computation.53 | loop fusion | bytes 3145740 | tf_op jit(solution)/shard_map/dynamic_slice | solution.py:279
  2.4 8.8 %collective-permute-start.3 = (bf16[1,64,4096]{2,1,0:T(8,128)(2,1)S(1)}, bf16[1,64,4096]{2,1,0:T(8,128)(2,1)S(1)}, u32[]{:S(2)}, u32[]{:S(2)}) collective-permute-start(bf16[1,64,4096]{2,1,0:T(8,128)(2,1)S(1)} %get-tuple-element.7), channel_id=1, source_target_pairs={{62,0},{3,1},{0,2},{37,3},{34,4},{7,5},{4,6},{41,7},{38,8},{11,9},... | collective-permute-start | bytes 1572872 | tf_op jit(solution)/shard_map/ppermute | solution.py:263
  11.2 0.0 collective-permute-start.1
  11.2 0.9 %collective-permute-start = (bf16[1,64,4096]{2,1,0:T(8,128)(2,1)S(1)}, bf16[1,64,4096]{2,1,0:T(8,128)(2,1)S(1)}, u32[]{:S(2)}, u32[]{:S(2)}) collective-permute-start(bf16[1,64,4096]{2,1,0:T(8,128)(2,1)S(1)} %get-tuple-element.7), channel_id=1, source_target_pairs={{1,0},{0,1},{3,2},{2,3},{5,4},{4,5},{7,6},{6,7},{9,8},{8,9},{11,10... | collective-permute-start | bytes 1572872 | tf_op jit(solution)/shard_map/ppermute | solution.py:263
  12.2 7.9 %collective-permute-done.1.pb_hbm = bf16[1,64,4096]{2,1,0:T(8,128)(2,1)S(1)} collective-permute-done((bf16[1,64,4096]{2,1,0:T(8,128)(2,1)S(1)}, bf16[1,64,4096]{2,1,0:T(8,128)(2,1)S(1)}, u32[]{:S(2)}, u32[]{:S(2)}) %collective-permute-start.1) | collective-permute-done | bytes 524320 | tf_op jit(solution)/shard_map/ppermute | solution.py:263
  20.1 0.0 copy-start.2
  20.1 4.0 %collective-permute-start.2 = (bf16[1,64,4096]{2,1,0:T(8,128)(2,1)S(1)}, bf16[1,64,4096]{2,1,0:T(8,128)(2,1)S(1)}, u32[]{:S(2)}, u32[]{:S(2)}) collective-permute-start(bf16[1,64,4096]{2,1,0:T(8,128)(2,1)S(1)} %collective-permute-done.1.pb_hbm), channel_id=1, source_target_pairs={{1,0},{0,1},{3,2},{2,3},{5,4},{4,5},{7,6},{6,7},{9,8},{8,9},{11,10... | collective-permute-start | bytes 1572872 | tf_op jit(solution)/shard_map/ppermute | solution.py:263
  24.2 3.7 %fusion.kt_hbm = f32[32,128,128]{2,1,0:T(8,128)S(1)} fusion(s32[128]{0:T(128)S(1)} %get-tuple-element.14, s32[128]{0:T(128)S(1)} %get-tuple-element.25, s32[32]{0:T(128)S(1)} %get-tuple-element.18, s32[32]{0:T(128)S(1)} %get-tuple-element.22, s32[128]{0:T(128)S(1)} %get-tuple-element.15, s32[128]{0:T(128)S(1)} %get-tuple-element.21, ...), kind=kLoop, calls=%fused_computation.19 | loop fusion | flops 35127296 | bytes 2103488 | tf_op jit(solution)/shard_map/mul | solution.py:65
  27.9 0.0 copy-start
  27.9 0.0 collective-permute-done.3.pd_hbm
  27.9 0.0 copy-start.1
  27.9 0.0 collective-permute-done.pa_hbm
  27.9 0.0 copy-start.3
  27.9 0.0 collective-permute-done.2.pc_hbm
  27.9 0.0 copy-start.4
  27.9 0.0 copy-done.5
  28.0 11.2 %pair_row.2 = bf16[64,4224]{1,0:T(8,128)(2,1)} custom-call(bf16[1,64,4096]{2,1,0:T(8,128)(2,1)S(1)} %get-tuple-element.6.own_hbm, bf16[1,64,4096]{2,1,0:T(8,128)(2,1)S(1)} %collective-permute-done.pa_hbm, bf16[1,64,4096]{2,1,0:T(8,128)(2,1)S(1)} %collective-permute-done.1.pb_hbm, bf16[1,64,4096]{2,1,0:T(8,128)(2,1)S(1)} %collective-permute-done.2.pc_hbm, ...), custom_call_target="tpu_custom_call" | custom-call | flops 6979321856 | bytes 8388608 | tf_op jit(solution)/shard_map/pair_row/pallas_call | solution.py:196
  39.2 0.0 copy-done.2
  39.2 0.0 copy-done
  39.2 0.0 copy-done.1
  39.2 0.0 copy-done.3
  39.2 0.0 copy-done.4
  39.2 4.0 %all-to-all-start = ((bf16[8,8,4224]{2,1,0:T(8,128)(2,1)}), bf16[8,8,4224]{2,1,0:T(8,128)(2,1)S(1)}, u32[]{:S(2)}, u32[]{:S(2)}) async-start(bf16[8,8,4224]{2,1,0:T(8,128)(2,1)} %bitcast), calls=%async_computation | async-start | bytes 1081344 | tf_op jit(solution)/shard_map/all_to_all | solution.py:267
  43.3 12.2 %pair_row.3 = bf16[64,4224]{1,0:T(8,128)(2,1)} custom-call(bf16[1,64,4096]{2,1,0:T(8,128)(2,1)} %get-tuple-element.5.own_hbm, bf16[1,64,4096]{2,1,0:T(8,128)(2,1)} %copy-done.3, bf16[1,64,4096]{2,1,0:T(8,128)(2,1)} %copy-done.2, bf16[1,64,4096]{2,1,0:T(8,128)(2,1)} %copy-done.4, bf16[1,64,4096]{2,1,0:T(8,128)(2,1)} %copy-done.1, ...), custom_call_target="tpu_custom_call" | custom-call | flops 6979321856 | bytes 8388608 | tf_op jit(solution)/shard_map/pair_row/pallas_call | solution.py:196
  55.4 0.0 all-to-all-done.refs_0_
  55.4 6.7 %all-to-all-start.1 = ((bf16[8,8,4224]{2,1,0:T(8,128)(2,1)}), bf16[8,8,4224]{2,1,0:T(8,128)(2,1)S(1)}, u32[]{:S(2)}, u32[]{:S(2)}) async-start(bf16[8,8,4224]{2,1,0:T(8,128)(2,1)} %bitcast.2), calls=%async_computation.1 | async-start | bytes 1081344 | tf_op jit(solution)/shard_map/all_to_all | solution.py:267
  62.1 0.4 gathered.2.refs_0_
  62.5 10.3 %all-to-all-done.1.refs_1_ = bf16[8,8,4224]{2,1,0:T(8,128)(2,1)S(1)} async-done(((bf16[8,8,4224]{2,1,0:T(8,128)(2,1)}), bf16[8,8,4224]{2,1,0:T(8,128)(2,1)S(1)}, u32[]{:S(2)}, u32[]{:S(2)}) %all-to-all-start.1) | async-done | bytes 540704 | tf_op jit(solution)/shard_map/all_to_all | solution.py:267
  72.8 1.3 %gathered.3 = f32[4,8,4096]{2,1,0:T(8,128)} custom-call(f32[2,8,4096]{2,1,0:T(8,128)S(1)} %gathered.2.refs_0_, bf16[8,8,4224]{2,1,0:T(8,128)(2,1)S(1)} %all-to-all-done.1.refs_1_), custom_call_target="tpu_custom_call" | custom-call | flops 4194304 | bytes 1048576 | tf_op jit(solution)/shard_map/gathered/pallas_call | solution.py:241
  (11 shorter events, 0.1 us)
Async XLA Ops:
  0.0 27.9 %copy-start.5 = (bf16[7,256,256]{2,1,0:T(8,128)(2,1)S(1)}, bf16[7,256,256]{2,1,0:T(8,128)(2,1)}, u32[]{:S(2)}) copy-start(bf16[7,256,256]{2,1,0:T(8,128)(2,1)} %constant.149.clone.tabs_hbm) | copy-start | bytes 2752516
  2.4 25.5 %collective-permute-start.3 = (bf16[1,64,4096]{2,1,0:T(8,128)(2,1)S(1)}, bf16[1,64,4096]{2,1,0:T(8,128)(2,1)S(1)}, u32[]{:S(2)}, u32[]{:S(2)}) collective-permute-start(bf16[1,64,4096]{2,1,0:T(8,128)(2,1)S(1)} %get-tuple-element.7), channel_id=1, source_target_pairs={{62,0},{3,1},{0,2},{37,3},{34,4},{7,5},{4,6},{41,7},{38,8},{11,9},... | collective-permute-start | bytes 1572872 | tf_op jit(solution)/shard_map/ppermute | solution.py:263
  11.2 8.9 %collective-permute-start.1 = (bf16[1,64,4096]{2,1,0:T(8,128)(2,1)S(1)}, bf16[1,64,4096]{2,1,0:T(8,128)(2,1)S(1)}, u32[]{:S(2)}, u32[]{:S(2)}) collective-permute-start(bf16[1,64,4096]{2,1,0:T(8,128)(2,1)S(1)} %get-tuple-element.7), channel_id=1, source_target_pairs={{63,0},{2,1},{1,2},{36,3},{35,4},{6,5},{5,6},{40,7},{39,8},{10,9},... | collective-permute-start | bytes 1572872 | tf_op jit(solution)/shard_map/ppermute | solution.py:263
  11.2 16.7 %collective-permute-start = (bf16[1,64,4096]{2,1,0:T(8,128)(2,1)S(1)}, bf16[1,64,4096]{2,1,0:T(8,128)(2,1)S(1)}, u32[]{:S(2)}, u32[]{:S(2)}) collective-permute-start(bf16[1,64,4096]{2,1,0:T(8,128)(2,1)S(1)} %get-tuple-element.7), channel_id=1, source_target_pairs={{1,0},{0,1},{3,2},{2,3},{5,4},{4,5},{7,6},{6,7},{9,8},{8,9},{11,10... | collective-permute-start | bytes 1572872 | tf_op jit(solution)/shard_map/ppermute | solution.py:263
  20.1 19.0 %copy-start.2 = (bf16[1,64,4096]{2,1,0:T(8,128)(2,1)}, bf16[1,64,4096]{2,1,0:T(8,128)(2,1)S(1)}, u32[]{:S(2)}) copy-start(bf16[1,64,4096]{2,1,0:T(8,128)(2,1)S(1)} %collective-permute-done.1.pb_hbm) | copy-start | bytes 1572868
  20.1 7.8 %collective-permute-start.2 = (bf16[1,64,4096]{2,1,0:T(8,128)(2,1)S(1)}, bf16[1,64,4096]{2,1,0:T(8,128)(2,1)S(1)}, u32[]{:S(2)}, u32[]{:S(2)}) collective-permute-start(bf16[1,64,4096]{2,1,0:T(8,128)(2,1)S(1)} %collective-permute-done.1.pb_hbm), channel_id=1, source_target_pairs={{1,0},{0,1},{3,2},{2,3},{5,4},{4,5},{7,6},{6,7},{9,8},{8,9},{11,10... | collective-permute-start | bytes 1572872 | tf_op jit(solution)/shard_map/ppermute | solution.py:263
  27.9 11.3 %copy-start = (f32[32,128,128]{2,1,0:T(8,128)}, f32[32,128,128]{2,1,0:T(8,128)S(1)}, u32[]{:S(2)}) copy-start(f32[32,128,128]{2,1,0:T(8,128)S(1)} %fusion.kt_hbm) | copy-start | bytes 6291460
  27.9 11.3 %copy-start.1 = (bf16[1,64,4096]{2,1,0:T(8,128)(2,1)}, bf16[1,64,4096]{2,1,0:T(8,128)(2,1)S(1)}, u32[]{:S(2)}) copy-start(bf16[1,64,4096]{2,1,0:T(8,128)(2,1)S(1)} %collective-permute-done.3.pd_hbm) | copy-start | bytes 1572868
  27.9 11.3 %copy-start.3 = (bf16[1,64,4096]{2,1,0:T(8,128)(2,1)}, bf16[1,64,4096]{2,1,0:T(8,128)(2,1)S(1)}, u32[]{:S(2)}) copy-start(bf16[1,64,4096]{2,1,0:T(8,128)(2,1)S(1)} %collective-permute-done.pa_hbm) | copy-start | bytes 1572868
  27.9 11.3 %copy-start.4 = (bf16[1,64,4096]{2,1,0:T(8,128)(2,1)}, bf16[1,64,4096]{2,1,0:T(8,128)(2,1)S(1)}, u32[]{:S(2)}) copy-start(bf16[1,64,4096]{2,1,0:T(8,128)(2,1)S(1)} %collective-permute-done.2.pc_hbm) | copy-start | bytes 1572868
  39.2 16.2 %all-to-all-start = ((bf16[8,8,4224]{2,1,0:T(8,128)(2,1)}), bf16[8,8,4224]{2,1,0:T(8,128)(2,1)S(1)}, u32[]{:S(2)}, u32[]{:S(2)}) async-start(bf16[8,8,4224]{2,1,0:T(8,128)(2,1)} %bitcast), calls=%async_computation | async-start | bytes 1081344 | tf_op jit(solution)/shard_map/all_to_all | solution.py:267
  55.4 17.4 %all-to-all-start.1 = ((bf16[8,8,4224]{2,1,0:T(8,128)(2,1)}), bf16[8,8,4224]{2,1,0:T(8,128)(2,1)S(1)}, u32[]{:S(2)}, u32[]{:S(2)}) async-start(bf16[8,8,4224]{2,1,0:T(8,128)(2,1)} %bitcast.2), calls=%async_computation.1 | async-start | bytes 1081344 | tf_op jit(solution)/shard_map/all_to_all | solution.py:267
